TPU v7x, 32 devices: a whole 2x2x4 slice. The times are simulated.
32 devices in a mesh: row: 8 (over y, x, core), col: 4 (over z).
Axes of the slice: x: 2, y: 2, z: 4, core: 2. Of those that a mesh axis runs over, the one named last changes fastest.
Arguments:
- start_modes: float32 [32, 131072], P(None, ('row', 'col')), may hold values from -6 to 6
- energies: float32 [131072], P(('row', 'col')), may hold values from -0.5 to 0.5
- coupling: float32 [2048, 20, 4096], P('row', 'col'), may hold values from -0.078125 to 0.078125
- pattern: int32 [2048, 20], P('row', 'col'), may hold values from 0 to 2047, as said below
Outputs:
- filtered: float32 [32, 131072], P(None, ('row', 'col'))
- previous: float32 [32, 131072], P(None, ('row', 'col'))
Inputs may be any that keep to these rules, and one draw needn't show every extreme that they name: In block row i, the 5 entries pattern[i, c * 5] to pattern[i, c * 5 + 4] are distinct block columns j with (j // 64) % 4 == c.
All inputs are finite; a program needn't handle non-finite values.
Results may differ from a plain program's by a relative error of at most 0.0001.
Values sent between devices are 32-bit elements; how exact they have to be, the bound alone decides.
A program may use at most 192 MiB of HBM per device.

v0:
```python
import jax
import jax.numpy as jnp
from jax import lax
from jax.sharding import PartitionSpec as P

BLOCK = 64
DEGREE = 3


def shards(start_modes, energies, coupling, pattern):
    col_count = lax.axis_size("col")
    mode_count, piece_len = start_modes.shape
    per_piece = piece_len // BLOCK
    rows_here, slot_count = pattern.shape
    piece_ids = pattern // per_piece
    places = piece_ids // col_count * per_piece + pattern % per_piece
    block_mats = coupling.reshape(rows_here, slot_count, BLOCK, BLOCK)

    def coupled(gathered, row_count):
        blocks = gathered.reshape(mode_count, -1, BLOCK)
        sub_mats = block_mats
        picked = jnp.take(blocks, places.reshape(-1), axis=1).reshape(
            mode_count, row_count, per_piece, slot_count, BLOCK
        )
        sub_mats = sub_mats.reshape(row_count, per_piece, slot_count, BLOCK, BLOCK)
        result = jnp.einsum("mqksb,qksab->qmka", picked, sub_mats, precision=lax.Precision.HIGHEST)
        return result.reshape(row_count, mode_count, per_piece * BLOCK)

    def operate(vector):
        gathered = lax.all_gather(vector, "row", axis=1, tiled=True)
        shares_row = lax.psum_scatter(
            coupled(gathered, col_count), "col", scatter_dimension=0, tiled=True
        )[0]
        return energies[None, :] * vector + shares_row

    previous = start_modes
    current = operate(start_modes)
    for degree in range(DEGREE - 1):
        upcoming = 2.0 * operate(current) - previous
        previous = current
        current = upcoming
    return (current, previous)


def solution(mesh):
    in_specs = (P(None, ("row", "col")), P(("row", "col")), P("row", "col", None), P("row", "col"))
    out_specs = (P(None, ("row", "col")), P(None, ("row", "col")))
    return jax.shard_map(shards, mesh=mesh, in_specs=in_specs, out_specs=out_specs, check_vma=False)
```

profile of v0, /device:TPU:0, one launch (start us, length us, event | category | flops | bytes accessed | tf_op | source)
XLA Modules:
  0.0 585.5 jit_solution(14820434715844887029)
XLA Ops:
  7.2 0.0 all-gather.4.cloned.1.call-start
  7.2 0.7 all-gather.4.cloned.1.call-update
  7.9 0.0 reduce-scatter.4.cloned.1.call-start
  7.9 0.7 fusion.21
  8.7 0.1 copy.12
  8.8 0.2 reshape.43
  9.0 33.5 %reshape_reshape.2 = f32[4,64,5,64,64]{4,3,1,0,2:T(8,128)} reshape(f32[256,5,4096]{2,0,1:T(8,128)} %param.8) | data formatting | bytes 41943040 | tf_op jit(solution)/shard_map/reshape;reshape | solution.py:25
  42.5 6.7 %all-gather.4.cloned.1.call-done = f32[32,32768]{1,0:T(8,128)} async-done(((f32[32,4096]{1,0:T(8,128)}), f32[32,32768]{1,0:T(8,128)}) %all-gather.4.cloned.1.call-update) | async-done | bytes 4194320 | tf_op jit(solution)/shard_map/all_gather | solution.py:30
  49.2 7.3 %reshape.42 = f32[32,512,64]{2,1,0:T(8,128)} reshape(f32[32,32768]{1,0:T(8,128)} %all-gather.4.cloned.1.call-done) | data formatting | bytes 8388608 | tf_op jit(solution)/shard_map/reshape | solution.py:20
  56.5 11.5 %copy.13 = f32[32,512,64]{2,0,1:T(8,128)} copy(f32[32,512,64]{2,1,0:T(8,128)} %reshape.42) | data formatting | bytes 8388608 | tf_op jit(solution)/shard_map/reshape | solution.py:20
  68.0 13.0 %gather_fusion = f32[1280,32,64]{2,1,0:T(8,128)} fusion(f32[32,512,64]{2,0,1:T(8,128)} %copy.13, s32[2048]{0:T(1024)S(1)} %pad_clamp_fusion), kind=kCustom, calls=%fused_computation.clone | custom fusion | bytes 20976640 | tf_op jit(solution)/shard_map/jit(_take)/gather | solution.py:22
  81.0 17.1 %broadcast_select_fusion.2 = f32[1280,32,64]{2,1,0:T(8,128)} fusion(f32[1280,32,64]{2,1,0:T(8,128)} %gather_fusion, pred[1280]{0:T(1024)(128)(4,1)S(1)} %compare_and_fusion), kind=kLoop, calls=%fused_computation.11 | loop fusion | flops 2621440 | bytes 20972800 | tf_op jit(solution)/shard_map/jit(_take)/select_n | solution.py:22
  98.1 48.6 %fusion.6 = f32[4,32,64,64]{3,1,2,0:T(8,128)S(1)} fusion(f32[32,4,64,5,64]{4,0,3,2,1:T(8,128)} %bitcast.50, f32[4,64,5,64,64]{4,3,1,0,2:T(8,128)} %reshape_reshape.2), kind=kOutput, calls=%fused_computation.12 | convolution fusion | flops 2013265920 | bytes 33554432 | tf_op jit(solution)/shard_map/mqksb,qksab->qmka/dot_general | solution.py:26
  146.7 4.4 copy.15
  151.0 4.8 reshape.45
  155.8 0.0 reduce-scatter.4.cloned.1.call-update
  155.8 0.0 all-gather.6.cloned.1.call-start
  155.9 43.7 %reduce-scatter.4.cloned.1.call-done = f32[1,32,4096]{2,1,0:T(8,128)} async-done(((f32[4,32,4096]{2,1,0:T(8,128)}), f32[1,32,4096]{2,1,0:T(8,128)}) %reduce-scatter.4.cloned.1.call-update) | async-done | bytes 524304 | tf_op jit(solution)/shard_map/reduce_scatter | solution.py:31
  199.6 0.0 copy-done.3
  199.6 1.9 bitcast_add_fusion.2
  201.5 0.0 all-gather.6.cloned.1.call-update
  201.5 0.0 reduce-scatter.6.cloned.1.call-start
  201.6 36.3 %all-gather.6.cloned.1.call-done = f32[32,32768]{1,0:T(8,128)} async-done(((f32[32,4096]{1,0:T(8,128)}), f32[32,32768]{1,0:T(8,128)}) %all-gather.6.cloned.1.call-update) | async-done | bytes 4194320 | tf_op jit(solution)/shard_map/all_gather | solution.py:30
  237.9 7.3 %reshape.46 = f32[32,512,64]{2,1,0:T(8,128)} reshape(f32[32,32768]{1,0:T(8,128)} %all-gather.6.cloned.1.call-done) | data formatting | bytes 8388608 | tf_op jit(solution)/shard_map/reshape | solution.py:20
  245.2 11.5 %copy.16 = f32[32,512,64]{2,0,1:T(8,128)} copy(f32[32,512,64]{2,1,0:T(8,128)} %reshape.46) | data formatting | bytes 8388608 | tf_op jit(solution)/shard_map/reshape | solution.py:20
  256.7 13.0 %gather_fusion.1 = f32[1280,32,64]{2,1,0:T(8,128)} fusion(f32[32,512,64]{2,0,1:T(8,128)} %copy.16, s32[2048]{0:T(1024)S(1)} %pad_clamp_fusion), kind=kCustom, calls=%fused_computation.1.clone | custom fusion | bytes 20976640 | tf_op jit(solution)/shard_map/jit(_take)/gather | solution.py:22
  269.7 17.1 %broadcast_select_fusion.1 = f32[1280,32,64]{2,1,0:T(8,128)} fusion(f32[1280,32,64]{2,1,0:T(8,128)} %gather_fusion.1, pred[1280]{0:T(1024)(128)(4,1)S(1)} %compare_and_fusion), kind=kLoop, calls=%fused_computation.10 | loop fusion | flops 2621440 | bytes 20972800 | tf_op jit(solution)/shard_map/jit(_take)/select_n | solution.py:22
  286.8 48.5 %fusion.9 = f32[4,32,64,64]{3,1,2,0:T(8,128)S(1)} fusion(f32[32,4,64,5,64]{4,0,3,2,1:T(8,128)} %bitcast.51, f32[4,64,5,64,64]{4,3,1,0,2:T(8,128)} %reshape_reshape.2), kind=kOutput, calls=%fused_computation.13 | convolution fusion | flops 2013265920 | bytes 33554432 | tf_op jit(solution)/shard_map/mqksb,qksab->qmka/dot_general | solution.py:26
  335.3 4.4 copy.18
  339.7 4.8 reshape.48
  344.4 0.0 reduce-scatter.6.cloned.1.call-update
  344.5 0.0 all-gather.8.cloned.1.call-start
  344.5 43.7 %reduce-scatter.6.cloned.1.call-done = f32[1,32,4096]{2,1,0:T(8,128)} async-done(((f32[4,32,4096]{2,1,0:T(8,128)}), f32[1,32,4096]{2,1,0:T(8,128)}) %reduce-scatter.6.cloned.1.call-update) | async-done | bytes 524304 | tf_op jit(solution)/shard_map/reduce_scatter | solution.py:31
  388.2 0.0 copy-done
  388.2 1.9 fusion.18
  390.2 0.0 all-gather.8.cloned.1.call-update
  390.2 0.0 reduce-scatter.8.cloned.1.call-start
  390.3 36.1 %all-gather.8.cloned.1.call-done = f32[32,32768]{1,0:T(8,128)} async-done(((f32[32,4096]{1,0:T(8,128)}), f32[32,32768]{1,0:T(8,128)}) %all-gather.8.cloned.1.call-update) | async-done | bytes 4194320 | tf_op jit(solution)/shard_map/all_gather | solution.py:30
  426.4 7.3 %reshape.49 = f32[32,512,64]{2,1,0:T(8,128)} reshape(f32[32,32768]{1,0:T(8,128)} %all-gather.8.cloned.1.call-done) | data formatting | bytes 8388608 | tf_op jit(solution)/shard_map/reshape | solution.py:20
  433.7 11.5 %copy.19 = f32[32,512,64]{2,0,1:T(8,128)} copy(f32[32,512,64]{2,1,0:T(8,128)} %reshape.49) | data formatting | bytes 8388608 | tf_op jit(solution)/shard_map/reshape | solution.py:20
  445.2 13.0 %gather_fusion.2 = f32[1280,32,64]{2,1,0:T(8,128)} fusion(f32[32,512,64]{2,0,1:T(8,128)} %copy.19, s32[2048]{0:T(1024)S(1)} %pad_clamp_fusion), kind=kCustom, calls=%fused_computation.2.clone | custom fusion | bytes 20976640 | tf_op jit(solution)/shard_map/jit(_take)/gather | solution.py:22
  458.2 17.1 %broadcast_select_fusion = f32[1280,32,64]{2,1,0:T(8,128)} fusion(f32[1280,32,64]{2,1,0:T(8,128)} %gather_fusion.2, pred[1280]{0:T(1024)(128)(4,1)S(1)} %compare_and_fusion), kind=kLoop, calls=%fused_computation.9 | loop fusion | flops 2621440 | bytes 20972800 | tf_op jit(solution)/shard_map/jit(_take)/select_n | solution.py:22
  475.3 48.3 %fusion.12 = f32[4,32,64,64]{3,1,2,0:T(8,128)S(1)} fusion(f32[32,4,64,5,64]{4,0,3,2,1:T(8,128)} %bitcast.49, f32[4,64,5,64,64]{4,3,1,0,2:T(8,128)} %reshape_reshape.2), kind=kOutput, calls=%fused_computation.14 | convolution fusion | flops 2013265920 | bytes 33554432 | tf_op jit(solution)/shard_map/mqksb,qksab->qmka/dot_general | solution.py:26
  523.6 4.4 copy.21
  527.9 4.8 reshape.51
  532.7 0.0 reduce-scatter.8.cloned.1.call-update
  532.7 43.8 %reduce-scatter.8.cloned.1.call-done = f32[1,32,4096]{2,1,0:T(8,128)} async-done(((f32[4,32,4096]{2,1,0:T(8,128)}), f32[1,32,4096]{2,1,0:T(8,128)}) %reduce-scatter.8.cloned.1.call-update) | async-done | bytes 524304 | tf_op jit(solution)/shard_map/reduce_scatter | solution.py:31
  576.5 1.9 fusion.16
  (9 shorter events, 0.0 us)
Async XLA Ops:
  7.2 42.1 %all-gather.4.cloned.1.call-start = ((), (), s32[]{:S(2)}) async-start(), calls=%async_computation.3 | async-start | bytes 4718592 | tf_op jit(solution)/shard_map/all_gather | solution.py:30
  7.9 191.7 %reduce-scatter.4.cloned.1.call-start = ((), (), s32[]{:S(2)}) async-start(), calls=%async_computation.4 | async-start | bytes 2621440 | tf_op jit(solution)/shard_map/reduce_scatter | solution.py:31
  98.1 101.5 %copy-start.1 = (f32[32,4096]{1,0:T(8,128)S(1)}, f32[32,4096]{1,0:T(8,128)}, u32[]{:S(2)}) copy-start(f32[32,4096]{1,0:T(8,128)} %param.6) | copy-start | bytes 1572868
  98.1 101.5 %copy-start.3 = (f32[4096]{0:T(1024)S(1)}, f32[4096]{0:T(1024)}, u32[]{:S(2)}) copy-start(f32[4096]{0:T(1024)} %param.7) | copy-start | bytes 49156
  155.8 82.1 %all-gather.6.cloned.1.call-start = ((), (), s32[]{:S(2)}) async-start(), calls=%async_computation.5 | async-start | bytes 4718592 | tf_op jit(solution)/shard_map/all_gather | solution.py:30
  201.5 186.7 %reduce-scatter.6.cloned.1.call-start = ((), (), s32[]{:S(2)}) async-start(), calls=%async_computation.6 | async-start | bytes 2621440 | tf_op jit(solution)/shard_map/reduce_scatter | solution.py:31
  286.8 101.5 %copy-start = (f32[32,4096]{1,0:T(8,128)S(1)}, f32[32,4096]{1,0:T(8,128)}, u32[]{:S(2)}) copy-start(f32[32,4096]{1,0:T(8,128)} %bitcast_add_fusion.2) | copy-start | bytes 1572868
  344.5 81.9 %all-gather.8.cloned.1.call-start = ((), (), s32[]{:S(2)}) async-start(), calls=%async_computation.7 | async-start | bytes 4718592 | tf_op jit(solution)/shard_map/all_gather | solution.py:30
  390.2 186.3 %reduce-scatter.8.cloned.1.call-start = ((), (), s32[]{:S(2)}) async-start(), calls=%async_computation.8 | async-start | bytes 2621440 | tf_op jit(solution)/shard_map/reduce_scatter | solution.py:31
  475.3 101.3 %copy-start.2 = (f32[32,4096]{1,0:T(8,128)S(1)}, f32[32,4096]{1,0:T(8,128)}, u32[]{:S(2)}) copy-start(f32[32,4096]{1,0:T(8,128)} %fusion.18) | copy-start | bytes 1572868
Sparse Core Ops, SparseCore 0:
  9.9 39.2 all-gather.3
  155.9 43.6 reduce-scatter.3
  202.1 35.7 all-gather.5
  344.6 43.6 reduce-scatter.5
  390.6 35.7 all-gather.7
  532.8 43.6 reduce-scatter.7
where the time goes:
time: 595 us; the launch traced here: 586 us
  waiting for transfers between devices  211 us (35%)
  local copies, waits for them, and re-layouts  157 us (26%)
  matrix products  145 us (24%)
  other arithmetic  57.8 us (10%)
  between operations  14.4 us (2%)
    dot_general x3, matrix products, coupled(): jnp.einsum('mqksb,qksab->qmka', picked, sub_mats, precision=lax.Precision...  145 us
    reduce_scatter x3, waiting for transfers between devices, operate(): lax.psum_scatter(coupled(gathered, col_count), 'col', scatter_dimension=0...  131 us
    all_gather x3, waiting for transfers between devices, operate(): gathered = lax.all_gather(vector, 'row', axis=1, tiled=True)  79.1 us
    reshape x6, local copies, waits for them, and re-layouts, coupled(): blocks = gathered.reshape(mode_count, -1, BLOCK)  56.4 us
    select_n x4, other arithmetic, coupled(): jnp.take(blocks, places.reshape(-1), axis=1)  51.3 us
    gather x3, local copies, waits for them, and re-layouts, coupled(): jnp.take(blocks, places.reshape(-1), axis=1)  39 us
    another operation x1, local copies, waits for them, and re-layouts, coupled(): sub_mats = sub_mats.reshape(row_count, per_piece, slot_count, BLOCK, BLOCK)  33.5 us
    reshape x3, local copies, waits for them, and re-layouts, coupled(): return result.reshape(row_count, mode_count, per_piece * BLOCK)  14.3 us
  transfers between devices with their start and end apart: 6, of which 6 were waited for; matrix products, arithmetic and copies ran while one was open for 6% of the time, Pallas kernels for 0%

commit v1 on v0

--- a/solution.py
+++ b/solution.py
@@ -2,9 +2,34 @@
 import jax.numpy as jnp
 from jax import lax
 from jax.sharding import PartitionSpec as P
+from jax.lax import axis_index, axis_size, ppermute
 
 BLOCK = 64
 DEGREE = 3
+
+
+def _attach_inputs(local_values, array_dim):
+    local_values = jnp.moveaxis(local_values, 0, array_dim)
+    fresh = local_values.shape
+    d_next = local_values.reshape(
+        *fresh[:array_dim], fresh[array_dim] * fresh[array_dim + 1], *fresh[array_dim + 2 :]
+    )
+    return d_next
+
+
+def part_local_data(z_in, named_axis):
+    reply = axis_size(named_axis)
+    moved = axis_index(named_axis)
+    placed, b_now = (reply, moved)
+    x_new, f_next = (z_in[None], 1)
+    while f_next < placed:
+        base_arr = ppermute(x_new, named_axis, [(kk, kk ^ f_next) for kk in range(placed)])
+        mid_arr = b_now & f_next == 0
+        answer = jnp.where(mid_arr, x_new, base_arr)
+        mixed_arr = jnp.where(mid_arr, base_arr, x_new)
+        x_new = jnp.concatenate([answer, mixed_arr])
+        f_next *= 2
+    return x_new
 
 
 def shards(start_modes, energies, coupling, pattern):
@@ -27,7 +52,8 @@
         return result.reshape(row_count, mode_count, per_piece * BLOCK)
 
     def operate(vector):
-        gathered = lax.all_gather(vector, "row", axis=1, tiled=True)
+        z_new = part_local_data(vector, "row")
+        gathered = _attach_inputs(z_new, 1)
         shares_row = lax.psum_scatter(
             coupled(gathered, col_count), "col", scatter_dimension=0, tiled=True
         )[0]

time: 595 us -> 729 us (1.23)
  waiting for transfers between devices: 211 us -> 310 us
  local copies, waits for them, and re-layouts: 157 us -> 173 us
  starting transfers between devices: 0.24 us -> 11.7 us
    ppermute x0 -> x9, waiting for transfers between devices: none -> 179 us  [part_local_data(): ppermute(x_new, named_axis, [(kk, kk ^ f_next) for kk in range(placed)])]
    all_gather x3 -> x0, waiting for transfers between devices: 79.1 us -> none  [operate(): gathered = lax.all_gather(vector, 'row', axis=1, tiled=True)]
    another operation x0 -> x6, local copies, waits for them, and re-layouts: none -> 58.7 us  [coupled(): blocks = gathered.reshape(mode_count, -1, BLOCK)]
    reshape x6 -> x0, local copies, waits for them, and re-layouts: 56.4 us -> none  [coupled(): blocks = gathered.reshape(mode_count, -1, BLOCK)]
    transpose x0 -> x3, local copies, waits for them, and re-layouts: none -> 13.5 us  [_attach_inputs(): local_values = jnp.moveaxis(local_values, 0, array_dim)]
    ppermute x0 -> x9, starting transfers between devices: none -> 11.6 us  [part_local_data(): ppermute(x_new, named_axis, [(kk, kk ^ f_next) for kk in range(placed)])]
  transfers between devices with their start and end apart: 6 -> 12, of which waited for: 6 -> 12; matrix products, arithmetic and copies ran while one was open for 6% -> 5% of each run, Pallas kernels for 0% -> 0%
where the time goes in v1:
time: 729 us; the launch traced here: 718 us
  waiting for transfers between devices  310 us (43%)
  local copies, waits for them, and re-layouts  173 us (24%)
  matrix products  145 us (20%)
  other arithmetic  64.7 us (9%)
  between operations  14.2 us (2%)
  starting transfers between devices  11.7 us (2%)
    ppermute x9, waiting for transfers between devices, part_local_data(): ppermute(x_new, named_axis, [(kk, kk ^ f_next) for kk in range(placed)])  179 us
    dot_general x3, matrix products, coupled(): jnp.einsum('mqksb,qksab->qmka', picked, sub_mats, precision=lax.Precision...  145 us
    reduce_scatter x3, waiting for transfers between devices, operate(): lax.psum_scatter(coupled(gathered, col_count), 'col', scatter_dimension=0...  131 us
    another operation x6, local copies, waits for them, and re-layouts, coupled(): blocks = gathered.reshape(mode_count, -1, BLOCK)  58.7 us
    select_n x4, other arithmetic, coupled(): jnp.take(blocks, places.reshape(-1), axis=1)  51.4 us
    gather x3, local copies, waits for them, and re-layouts, coupled(): jnp.take(blocks, places.reshape(-1), axis=1)  38.9 us
    another operation x1, local copies, waits for them, and re-layouts, coupled(): sub_mats = sub_mats.reshape(row_count, per_piece, slot_count, BLOCK, BLOCK)  33.5 us
  transfers between devices with their start and end apart: 12, of which 12 were waited for; matrix products, arithmetic and copies ran while one was open for 5% of the time, Pallas kernels for 0%

profile of v1, /device:TPU:0, one launch (start us, length us, event | category | flops | bytes accessed | tf_op | source)
XLA Modules:
  0.0 717.7 jit_solution(5311188670130811825)
XLA Ops:
  7.8 1.7 collective-permute-done
  10.7 2.9 collective-permute-start.1
  13.6 23.6 %collective-permute-done.1 = f32[2,32,4096]{2,1,0:T(8,128)} collective-permute-done((f32[2,32,4096]{2,1,0:T(8,128)S(1)}, f32[2,32,4096]{2,1,0:T(8,128)}, u32[]{:S(2)}, u32[]{:S(2)}) %collective-permute-start.1) | collective-permute-done | bytes 1048608 | tf_op jit(solution)/shard_map/ppermute | solution.py:26
  37.2 1.4 broadcast_select_fusion.14
  38.6 1.5 pad_maximum_fusion
  40.1 1.8 collective-permute-start.2
  42.2 33.5 %reshape_reshape.15 = f32[4,64,5,64,64]{4,3,1,0,2:T(8,128)} reshape(f32[256,5,4096]{2,0,1:T(8,128)} %param.8) | data formatting | bytes 41943040 | tf_op jit(solution)/shard_map/reshape;reshape | solution.py:50
  75.7 11.8 %collective-permute-done.2 = f32[4,32,4096]{2,1,0:T(8,128)} collective-permute-done((f32[4,32,4096]{2,1,0:T(8,128)}, f32[4,32,4096]{2,1,0:T(8,128)}, u32[]{:S(2)}, u32[]{:S(2)}) %collective-permute-start.2) | collective-permute-done | bytes 2097184 | tf_op jit(solution)/shard_map/ppermute | solution.py:26
  87.5 1.9 broadcast_select_fusion.8
  89.9 4.5 copy.10
  94.4 7.8 %reshape_reshape.14 = f32[32,512,64]{2,1,0:T(8,128)} reshape(f32[32,8,4096]{2,1,0:T(8,128)} %copy.10) | data formatting | bytes 8388608 | tf_op jit(solution)/shard_map/reshape;reshape | solution.py:45
  102.2 11.5 %copy.11 = f32[32,512,64]{2,0,1:T(8,128)} copy(f32[32,512,64]{2,1,0:T(8,128)} %reshape_reshape.14) | data formatting | bytes 8388608 | tf_op jit(solution)/shard_map/reshape;reshape | solution.py:45
  113.7 13.0 %gather_fusion = f32[1280,32,64]{2,1,0:T(8,128)} fusion(f32[32,512,64]{2,0,1:T(8,128)} %copy.11, s32[2048]{0:T(1024)S(1)} %pad_clamp_fusion), kind=kCustom, calls=%fused_computation.clone | custom fusion | bytes 20976640 | tf_op jit(solution)/shard_map/jit(_take)/gather | solution.py:47
  126.7 17.2 %broadcast_select_fusion.2 = f32[1280,32,64]{2,1,0:T(8,128)} fusion(f32[1280,32,64]{2,1,0:T(8,128)} %gather_fusion, pred[1280]{0:T(1024)(128)(4,1)S(1)} %compare_and_fusion), kind=kLoop, calls=%fused_computation.11 | loop fusion | flops 2621440 | bytes 20972800 | tf_op jit(solution)/shard_map/jit(_take)/select_n | solution.py:47
  143.9 48.1 %fusion.6 = f32[4,32,64,64]{3,1,2,0:T(8,128)S(1)} fusion(f32[32,4,64,5,64]{4,0,3,2,1:T(8,128)} %bitcast.70, f32[4,64,5,64,64]{4,3,1,0,2:T(8,128)} %reshape_reshape.15), kind=kOutput, calls=%fused_computation.15 | convolution fusion | flops 2013265920 | bytes 33554432 | tf_op jit(solution)/shard_map/mqksb,qksab->qmka/dot_general | solution.py:51
  192.1 4.4 copy.13
  196.4 4.8 reshape.35
  201.3 44.9 %reduce-scatter.4.cloned.1.call-done = f32[1,32,4096]{2,1,0:T(8,128)} async-done(((f32[4,32,4096]{2,1,0:T(8,128)}), f32[1,32,4096]{2,1,0:T(8,128)}) %reduce-scatter.4.cloned.1.call-update) | async-done | bytes 524304 | tf_op jit(solution)/shard_map/reduce_scatter | solution.py:57
  247.5 1.9 collective-permute-done.3
  249.5 1.6 collective-permute-start.4
  251.1 23.7 %collective-permute-done.4 = f32[2,32,4096]{2,1,0:T(8,128)S(1)} collective-permute-done((f32[2,32,4096]{2,1,0:T(8,128)S(1)}, f32[2,32,4096]{2,1,0:T(8,128)S(1)}, u32[]{:S(2)}, u32[]{:S(2)}) %collective-permute-start.4) | collective-permute-done | bytes 1048608 | tf_op jit(solution)/shard_map/ppermute | solution.py:26
  275.1 1.6 collective-permute-start.5
  276.7 45.3 %collective-permute-done.5 = f32[4,32,4096]{2,1,0:T(8,128)S(1)} collective-permute-done((f32[4,32,4096]{2,1,0:T(8,128)S(1)}, f32[4,32,4096]{2,1,0:T(8,128)S(1)}, u32[]{:S(2)}, u32[]{:S(2)}) %collective-permute-start.5) | collective-permute-done | bytes 2097184 | tf_op jit(solution)/shard_map/ppermute | solution.py:26
  322.9 4.5 copy.14
  327.4 8.2 %reshape_reshape.16 = f32[32,512,64]{2,1,0:T(8,128)} reshape(f32[32,8,4096]{2,1,0:T(8,128)} %copy.14) | data formatting | bytes 8388608 | tf_op jit(solution)/shard_map/reshape;reshape | solution.py:45
  335.6 11.5 %copy.15 = f32[32,512,64]{2,0,1:T(8,128)} copy(f32[32,512,64]{2,1,0:T(8,128)} %reshape_reshape.16) | data formatting | bytes 8388608 | tf_op jit(solution)/shard_map/reshape;reshape | solution.py:45
  347.1 13.0 %gather_fusion.1 = f32[1280,32,64]{2,1,0:T(8,128)} fusion(f32[32,512,64]{2,0,1:T(8,128)} %copy.15, s32[2048]{0:T(1024)S(1)} %pad_clamp_fusion), kind=kCustom, calls=%fused_computation.1.clone | custom fusion | bytes 20976640 | tf_op jit(solution)/shard_map/jit(_take)/gather | solution.py:47
  360.0 17.1 %broadcast_select_fusion.1 = f32[1280,32,64]{2,1,0:T(8,128)} fusion(f32[1280,32,64]{2,1,0:T(8,128)} %gather_fusion.1, pred[1280]{0:T(1024)(128)(4,1)S(1)} %compare_and_fusion), kind=kLoop, calls=%fused_computation.10 | loop fusion | flops 2621440 | bytes 20972800 | tf_op jit(solution)/shard_map/jit(_take)/select_n | solution.py:47
  377.1 48.3 %fusion.9 = f32[4,32,64,64]{3,1,2,0:T(8,128)S(1)} fusion(f32[32,4,64,5,64]{4,0,3,2,1:T(8,128)} %bitcast.71, f32[4,64,5,64,64]{4,3,1,0,2:T(8,128)} %reshape_reshape.15), kind=kOutput, calls=%fused_computation.16 | convolution fusion | flops 2013265920 | bytes 33554432 | tf_op jit(solution)/shard_map/mqksb,qksab->qmka/dot_general | solution.py:51
  425.4 4.4 copy.17
  429.8 4.8 reshape.37
  434.7 43.0 %reduce-scatter.6.cloned.1.call-done = f32[1,32,4096]{2,1,0:T(8,128)} async-done(((f32[4,32,4096]{2,1,0:T(8,128)}), f32[1,32,4096]{2,1,0:T(8,128)}) %reduce-scatter.6.cloned.1.call-update) | async-done | bytes 524304 | tf_op jit(solution)/shard_map/reduce_scatter | solution.py:57
  477.6 1.2 fusion.18
  478.9 1.9 collective-permute-done.6
  480.9 1.5 collective-permute-start.7
  482.5 23.7 %collective-permute-done.7 = f32[2,32,4096]{2,1,0:T(8,128)S(1)} collective-permute-done((f32[2,32,4096]{2,1,0:T(8,128)S(1)}, f32[2,32,4096]{2,1,0:T(8,128)S(1)}, u32[]{:S(2)}, u32[]{:S(2)}) %collective-permute-start.7) | collective-permute-done | bytes 1048608 | tf_op jit(solution)/shard_map/ppermute | solution.py:26
  506.5 1.6 collective-permute-start.8
  508.1 45.3 %collective-permute-done.8 = f32[4,32,4096]{2,1,0:T(8,128)S(1)} collective-permute-done((f32[4,32,4096]{2,1,0:T(8,128)S(1)}, f32[4,32,4096]{2,1,0:T(8,128)S(1)}, u32[]{:S(2)}, u32[]{:S(2)}) %collective-permute-start.8) | collective-permute-done | bytes 2097184 | tf_op jit(solution)/shard_map/ppermute | solution.py:26
  554.3 4.5 copy.18
  558.8 8.2 %reshape_reshape.17 = f32[32,512,64]{2,1,0:T(8,128)} reshape(f32[32,8,4096]{2,1,0:T(8,128)} %copy.18) | data formatting | bytes 8388608 | tf_op jit(solution)/shard_map/reshape;reshape | solution.py:45
  567.0 11.5 %copy.19 = f32[32,512,64]{2,0,1:T(8,128)} copy(f32[32,512,64]{2,1,0:T(8,128)} %reshape_reshape.17) | data formatting | bytes 8388608 | tf_op jit(solution)/shard_map/reshape;reshape | solution.py:45
  578.5 13.0 %gather_fusion.2 = f32[1280,32,64]{2,1,0:T(8,128)} fusion(f32[32,512,64]{2,0,1:T(8,128)} %copy.19, s32[2048]{0:T(1024)S(1)} %pad_clamp_fusion), kind=kCustom, calls=%fused_computation.2.clone | custom fusion | bytes 20976640 | tf_op jit(solution)/shard_map/jit(_take)/gather | solution.py:47
  591.5 17.1 %broadcast_select_fusion = f32[1280,32,64]{2,1,0:T(8,128)} fusion(f32[1280,32,64]{2,1,0:T(8,128)} %gather_fusion.2, pred[1280]{0:T(1024)(128)(4,1)S(1)} %compare_and_fusion), kind=kLoop, calls=%fused_computation.9 | loop fusion | flops 2621440 | bytes 20972800 | tf_op jit(solution)/shard_map/jit(_take)/select_n | solution.py:47
  608.5 48.3 %fusion.12 = f32[4,32,64,64]{3,1,2,0:T(8,128)S(1)} fusion(f32[32,4,64,5,64]{4,0,3,2,1:T(8,128)} %bitcast.69, f32[4,64,5,64,64]{4,3,1,0,2:T(8,128)} %reshape_reshape.15), kind=kOutput, calls=%fused_computation.17 | convolution fusion | flops 2013265920 | bytes 33554432 | tf_op jit(solution)/shard_map/mqksb,qksab->qmka/dot_general | solution.py:51
  656.8 4.4 copy.21
  661.2 4.8 reshape.39
  666.0 43.0 %reduce-scatter.8.cloned.1.call-done = f32[1,32,4096]{2,1,0:T(8,128)} async-done(((f32[4,32,4096]{2,1,0:T(8,128)}), f32[1,32,4096]{2,1,0:T(8,128)}) %reduce-scatter.8.cloned.1.call-update) | async-done | bytes 524304 | tf_op jit(solution)/shard_map/reduce_scatter | solution.py:57
  709.0 2.0 fusion.16
  (41 shorter events, 6.6 us)
Async XLA Ops:
  7.2 239.1 %reduce-scatter.4.cloned.1.call-start = ((), (), s32[]{:S(2)}) async-start(), calls=%async_computation.3 | async-start | bytes 2621440 | tf_op jit(solution)/shard_map/reduce_scatter | solution.py:57
  7.2 2.3 collective-permute-start
  10.7 26.5 %collective-permute-start.1 = (f32[2,32,4096]{2,1,0:T(8,128)S(1)}, f32[2,32,4096]{2,1,0:T(8,128)}, u32[]{:S(2)}, u32[]{:S(2)}) collective-permute-start(f32[2,32,4096]{2,1,0:T(8,128)S(1)} %pad_maximum_fusion.3), channel_id=1, source_target_pairs={{0,8},{4,12},{8,0},{12,4},{16,24},{20,28},{24,16},{28,20},{1,9},{5... | collective-permute-start | bytes 3145736 | tf_op jit(solution)/shard_map/ppermute | solution.py:26
  13.6 28.2 %copy-start.4 = (s32[256,5]{0,1:T(8,128)S(1)}, s32[256,5]{0,1:T(8,128)}, u32[]{:S(2)}) copy-start(s32[256,5]{0,1:T(8,128)} %param.9) | copy-start | bytes 15364
  40.1 47.4 %collective-permute-start.2 = (f32[4,32,4096]{2,1,0:T(8,128)}, f32[4,32,4096]{2,1,0:T(8,128)}, u32[]{:S(2)}, u32[]{:S(2)}) collective-permute-start(f32[4,32,4096]{2,1,0:T(8,128)} %pad_maximum_fusion), channel_id=1, source_target_pairs={{0,16},{4,20},{8,24},{12,28},{16,0},{20,4},{24,8},{28,12},{1,17},{... | collective-permute-start | bytes 6291464 | tf_op jit(solution)/shard_map/ppermute | solution.py:26
  196.4 49.8 %copy-start = (f32[32,4096]{1,0:T(8,128)S(1)}, f32[32,4096]{1,0:T(8,128)}, u32[]{:S(2)}) copy-start(f32[32,4096]{1,0:T(8,128)} %param.6) | copy-start | bytes 1572868
  196.4 49.8 %copy-start.3 = (f32[4096]{0:T(1024)S(1)}, f32[4096]{0:T(1024)}, u32[]{:S(2)}) copy-start(f32[4096]{0:T(1024)} %param.7) | copy-start | bytes 49156
  201.3 276.4 %reduce-scatter.6.cloned.1.call-start = ((), (), s32[]{:S(2)}) async-start(), calls=%async_computation.4 | async-start | bytes 2621440 | tf_op jit(solution)/shard_map/reduce_scatter | solution.py:57
  247.4 2.0 collective-permute-start.3
  249.5 25.3 %collective-permute-start.4 = (f32[2,32,4096]{2,1,0:T(8,128)S(1)}, f32[2,32,4096]{2,1,0:T(8,128)S(1)}, u32[]{:S(2)}, u32[]{:S(2)}) collective-permute-start(f32[2,32,4096]{2,1,0:T(8,128)S(1)} %pad_maximum_fusion.4), channel_id=1, source_target_pairs={{0,8},{4,12},{8,0},{12,4},{16,24},{20,28},{24,16},{28,20},{1,9},{5... | collective-permute-start | bytes 3145736 | tf_op jit(solution)/shard_map/ppermute | solution.py:26
  275.1 46.9 %collective-permute-start.5 = (f32[4,32,4096]{2,1,0:T(8,128)S(1)}, f32[4,32,4096]{2,1,0:T(8,128)S(1)}, u32[]{:S(2)}, u32[]{:S(2)}) collective-permute-start(f32[4,32,4096]{2,1,0:T(8,128)S(1)} %pad_maximum_fusion.1), channel_id=1, source_target_pairs={{0,16},{4,20},{8,24},{12,28},{16,0},{20,4},{24,8},{28,12},{1,17},{... | collective-permute-start | bytes 6291464 | tf_op jit(solution)/shard_map/ppermute | solution.py:26
  429.8 47.9 %copy-start.1 = (f32[1,32,4096]{2,1,0:T(8,128)S(1)}, f32[1,32,4096]{2,1,0:T(8,128)}, u32[]{:S(2)}) copy-start(f32[1,32,4096]{2,1,0:T(8,128)} %reduce-scatter.4.cloned.1.call-done) | copy-start | bytes 1572868
  434.6 274.3 %reduce-scatter.8.cloned.1.call-start = ((), (), s32[]{:S(2)}) async-start(), calls=%async_computation.5 | async-start | bytes 2621440 | tf_op jit(solution)/shard_map/reduce_scatter | solution.py:57
  478.8 230.2 %copy-start.2 = (f32[32,4096]{1,0:T(8,128)}, f32[32,4096]{1,0:T(8,128)S(1)}, u32[]{:S(2)}) copy-start(f32[32,4096]{1,0:T(8,128)S(1)} %fusion.18) | copy-start | bytes 1572868
  478.8 2.0 collective-permute-start.6
  480.9 25.3 %collective-permute-start.7 = (f32[2,32,4096]{2,1,0:T(8,128)S(1)}, f32[2,32,4096]{2,1,0:T(8,128)S(1)}, u32[]{:S(2)}, u32[]{:S(2)}) collective-permute-start(f32[2,32,4096]{2,1,0:T(8,128)S(1)} %pad_maximum_fusion.5), channel_id=1, source_target_pairs={{0,8},{4,12},{8,0},{12,4},{16,24},{20,28},{24,16},{28,20},{1,9},{5... | collective-permute-start | bytes 3145736 | tf_op jit(solution)/shard_map/ppermute | solution.py:26
  506.5 46.9 %collective-permute-start.8 = (f32[4,32,4096]{2,1,0:T(8,128)S(1)}, f32[4,32,4096]{2,1,0:T(8,128)S(1)}, u32[]{:S(2)}, u32[]{:S(2)}) collective-permute-start(f32[4,32,4096]{2,1,0:T(8,128)S(1)} %pad_maximum_fusion.2), channel_id=1, source_target_pairs={{0,16},{4,20},{8,24},{12,28},{16,0},{20,4},{24,8},{28,12},{1,17},{... | collective-permute-start | bytes 6291464 | tf_op jit(solution)/shard_map/ppermute | solution.py:26
Sparse Core Ops, SparseCore 0:
  201.4 44.8 reduce-scatter.3
  434.7 42.8 reduce-scatter.5
  666.1 42.8 reduce-scatter.7
